TPU v7x, 32 devices: a whole 2x2x4 slice. The times are simulated.
32 devices in a mesh: group: 2 (over x), tile: 4 (over y, core), orient: 4 (over z).
Axes of the slice: x: 2, y: 2, z: 4, core: 2. Of those that a mesh axis runs over, the one named last changes fastest.
Arguments:
- micrograph: float32 [768, 1024], P('group', 'tile'), parts along dimension 0, may hold values from -30 to 30
- templates: float32 [4, 4, 128, 128], P('orient', 'tile'), may hold values from 0 to 0.0107421875
- orient_ids: int32 [4, 4], P('orient', 'tile'), may hold values from 0 to 15, as said below
- log_weight: float32 [16], replicated, may hold values from -2 to 2
- ice_mask: int32 [32, 64], P('group', 'tile'), parts along dimension 0, may hold values 0 or 1
Outputs:
- score_map: float32 [512, 1024], P(('group', 'orient'), 'tile'), parts along dimension 0
There are 2 independent parts, one for each index of `group`. A program takes and returns all parts, laid end to end along the dimension named above; an argument that names none is the same for every part. Nothing has to cross between parts.
Inputs may be any that keep to these rules, and one draw needn't show every extreme that they name: `orient_ids`: every slot holds a different orientation.
All inputs are finite; a program needn't handle non-finite values. No bound on the sum of `ice_mask` on one device may be relied on, other than what follows from the above.
Results may differ from a plain program's by a relative error of at most 0.00024.
Values sent between devices are 32-bit elements; how exact they have to be, the bound alone decides.
A program may use at most 64 MiB of HBM per device.

v0:
```python
import functools
import math

import jax
import jax.numpy as jnp
import numpy as np
from jax import lax
from jax.experimental import pallas as pl
from jax.experimental.pallas import tpu as pltpu
from jax.sharding import PartitionSpec as P

MBLK = 16
F32 = jnp.float32
BF16 = jnp.bfloat16
MESH = pl.DeviceIdType.MESH


def halves(table):
    table = jnp.asarray(table, F32) if isinstance(table, jax.Array) else table.astype(np.float32)
    high = table.astype(jnp.bfloat16)
    low = (table - high.astype(np.float32)).astype(jnp.bfloat16)
    return np.concatenate([high, low], axis=0)


def tables(patch):
    length = 2 * patch
    n = np.arange(length)[:, None]
    k = np.arange(patch)[None, :]
    theta = 2 * math.pi * ((n * (2 * k + 1)) % (2 * length)) / (2 * length)
    tx = np.concatenate([np.cos(theta), -np.sin(theta)], axis=1)
    back = theta[:patch].T
    ix = np.concatenate([np.cos(back), -np.sin(back)], axis=0) * (2.0 / length)
    m = np.arange(length)
    phi = 2 * math.pi * ((m[:, None] * m[None, :]) % length) / length
    c, s = np.cos(phi), np.sin(phi)
    ty = np.block([[c, s], [-s, c]])
    cp, sp = c[:, :patch], s[:, :patch]
    tt = np.block([[cp, sp], [-sp, cp]])
    ci, si = c[:patch], s[:patch]
    iy = np.block([[ci, -si], [si, ci]]) / length
    return tuple(halves(t) for t in (tx, ix, ty, tt, iy))


def split(value):
    high = value.astype(BF16)
    low = (value - high.astype(F32)).astype(BF16)
    return high, low


def dot(a, b):
    return jnp.dot(a, b, preferred_element_type=F32)


def left_table(table, high, low):
    rows = table.shape[0] // 2
    both = dot(table[...], high)
    return both[:rows] + both[rows:] + dot(table[:rows, :], low)


def right_table(value, table):
    rows = value.shape[0]
    depth = table.shape[0] // 2
    high, low = split(value)
    both = dot(jnp.concatenate([high, low], axis=0), table[:depth, :])
    return both[:rows] + both[rows:] + dot(high, table[depth:, :])


def kernel(
    tiles, orients, guard,
    mic, tpl, ids, logw, mask, tx, ix, ty, tt, iy,
    out,
    halo_l, halo_r, stack, wbuf, img, spec, scores, lse_out, lse_in, stats,
    halo_send, halo_recv, tpl_send, tpl_recv, w_send, w_recv,
    lse_send, lse_recv, st_send, st_recv,
):
    t = lax.axis_index("tile")
    o = lax.axis_index("orient")
    everyone = tiles * orients
    me = t * orients + o
    extent, side = mic.shape
    patch = tpl.shape[2]
    length = 2 * patch
    blocks = side // patch
    share = out.shape[0]

    barrier = pltpu.get_barrier_semaphore()

    def greet(k, carry):
        peer = lax.rem(me + k, everyone)
        pl.semaphore_signal(
            barrier, inc=1,
            device_id={"tile": peer // orients, "orient": lax.rem(peer, orients)},
            device_id_type=MESH,
        )
        return carry

    lax.fori_loop(1, everyone, greet, 0)

    wbuf[0] = jnp.full(wbuf.shape[1:], logw[ids[0, 0]], F32)
    stack[0] = tpl[0, 0]

    pl.semaphore_wait(barrier, everyone - 1)

    def halo_copy(src, dst, side_index, peer):
        return pltpu.make_async_remote_copy(
            src_ref=src, dst_ref=dst, send_sem=halo_send.at[side_index],
            recv_sem=halo_recv.at[side_index], device_id={"tile": peer}, device_id_type=MESH,
        )

    to_right = halo_copy(mic.at[:, side - patch:], halo_l, 0, lax.rem(t + 1, tiles))
    to_left = halo_copy(mic.at[:, :patch], halo_r, 1, lax.rem(t + tiles - 1, tiles))

    @pl.when(t < tiles - 1)
    def _():
        to_right.start()

    @pl.when(t > 0)
    def _():
        to_left.start()

    def tpl_copy(k):
        return pltpu.make_async_remote_copy(
            src_ref=tpl.at[0, 0], dst_ref=stack.at[k], send_sem=tpl_send.at[k],
            recv_sem=tpl_recv.at[k], device_id={"tile": lax.rem(t + k, tiles)},
            device_id_type=MESH,
        )

    def w_copy(k):
        return pltpu.make_async_remote_copy(
            src_ref=wbuf.at[0], dst_ref=wbuf.at[k], send_sem=w_send.at[k],
            recv_sem=w_recv.at[k], device_id={"tile": lax.rem(t + k, tiles)},
            device_id_type=MESH,
        )

    for k in range(1, tiles):
        tpl_copy(k).start()
    for k in range(1, tiles):
        w_copy(k).start()

    mask_rows, mask_cols = mask.shape
    row_id = lax.broadcasted_iota(jnp.int32, (share, mask_rows), 0) + o * share
    pick = lax.broadcasted_iota(jnp.int32, (share, mask_rows), 1)
    low_edge = pick * MBLK
    rows_of = jnp.where((row_id >= low_edge) & (row_id < low_edge + MBLK), 1.0, 0.0).astype(F32)
    col_id = lax.broadcasted_iota(jnp.int32, (mask_cols, side), 1)
    col_edge = lax.broadcasted_iota(jnp.int32, (mask_cols, side), 0) * MBLK
    cols_of = jnp.where((col_id >= col_edge) & (col_id < col_edge + MBLK), 1.0, 0.0).astype(F32)
    unmasked = 1.0 - dot(dot(rows_of, mask[...].astype(F32)), cols_of)

    @pl.when(t < tiles - 1)
    def _():
        to_right.wait_send()
        to_left.wait_recv()

    @pl.when(t == tiles - 1)
    def _():
        halo_r[...] = jnp.zeros(halo_r.shape, F32)

    @pl.when(t > 0)
    def _():
        to_left.wait_send()
        to_right.wait_recv()

    @pl.when(t == 0)
    def _():
        halo_l[...] = jnp.zeros(halo_l.shape, F32)

    rolled = [halo_l[...]] + [mic[:, b * patch:(b + 1) * patch] for b in range(blocks)] + [halo_r[...]]
    rolled = [pltpu.roll(part, guard, 1) for part in rolled]
    lane = lax.broadcasted_iota(jnp.int32, (extent, patch), 1)
    ext = [jnp.where(lane < guard, rolled[b], rolled[b + 1]) for b in range(blocks + 1)]
    real, imag = [], []
    for b in range(blocks):
        half = right_table(jnp.concatenate([ext[b], ext[b + 1]], axis=1), tx)
        real.append(half[:, :patch])
        imag.append(half[:, patch:])
    real_high, real_low = split(jnp.concatenate(real, axis=1))
    imag_high, imag_low = split(jnp.concatenate(imag, axis=1))
    for a in range(blocks):
        rows = slice(a * patch, a * patch + length)
        img[a] = left_table(
            ty,
            jnp.concatenate([real_high[rows], imag_high[rows]], axis=0),
            jnp.concatenate([real_low[rows], imag_low[rows]], axis=0),
        )

    tx_head = jnp.concatenate([tx[:patch, :], tx[length:length + patch, :]], axis=0)

    def one_template(k):
        half = right_table(stack[k], tx_head)
        high, low = split(jnp.concatenate([half[:, :patch], half[:, patch:]], axis=0))
        sp = left_table(tt, high, low)
        sr, si = sp[:length], sp[length:]
        wide_r = jnp.concatenate([sr] * blocks, axis=1)
        wide_i = jnp.concatenate([si] * blocks, axis=1)
        weight = wbuf[k][:1, :1]
        for a in range(blocks):
            ir, ii = img[a, :length, :], img[a, length:, :]
            cross = jnp.concatenate([ir * wide_r + ii * wide_i, ii * wide_r - ir * wide_i], axis=0)
            high, low = split(cross)
            mid = left_table(iy, high, low)
            pieces = jnp.concatenate(
                [
                    jnp.concatenate(
                        [mid[:patch, b * patch:(b + 1) * patch], mid[patch:, b * patch:(b + 1) * patch]],
                        axis=1,
                    )
                    for b in range(blocks)
                ],
                axis=0,
            )
            final = right_table(pieces, ix) + weight
            for b in range(blocks):
                scores[k, a * patch:(a + 1) * patch, b * patch:(b + 1) * patch] = final[
                    b * patch:(b + 1) * patch
                ]

    if tiles <= 4:
        for k in range(tiles):
            if k:
                tpl_copy(k).wait()
                w_copy(k).wait()
            one_template(k)
    else:
        for k in range(1, tiles):
            tpl_copy(k).wait()
            w_copy(k).wait()

        def step(k, carry):
            one_template(k)
            return carry

        lax.fori_loop(0, tiles, step, 0)

    def own_lse(owner):
        rows = pl.ds(pl.multiple_of(owner * share, share), share)
        top = scores[0, rows, :]
        for k in range(1, tiles):
            top = jnp.maximum(top, scores[k, rows, :])
        total = jnp.exp(scores[0, rows, :] - top)
        for k in range(1, tiles):
            total = total + jnp.exp(scores[k, rows, :] - top)
        return top + jnp.log(total)

    def lse_copy(k):
        return pltpu.make_async_remote_copy(
            src_ref=lse_out.at[k], dst_ref=lse_in.at[k], send_sem=lse_send.at[k],
            recv_sem=lse_recv.at[k], device_id={"orient": lax.rem(o + k, orients)},
            device_id_type=MESH,
        )

    for k in range(1, orients):
        lse_out[k] = own_lse(lax.rem(o + k, orients))
        lse_copy(k).start()
    mine = own_lse(o)
    for k in range(1, orients):
        lse_copy(k).wait()
    top = mine
    for k in range(1, orients):
        top = jnp.maximum(top, lse_in[k])
    total = jnp.exp(mine - top)
    for k in range(1, orients):
        total = total + jnp.exp(lse_in[k] - top)
    lse = top + jnp.log(total)

    def whole_sum(value):
        return jnp.sum(jnp.sum(value, axis=0, keepdims=True), axis=1, keepdims=True)

    count = whole_sum(unmasked)
    sum_here = whole_sum(unmasked * lse)
    mean_here = sum_here / jnp.maximum(count, 1.0)
    deviation = lse - mean_here
    squares = whole_sum(unmasked * deviation * deviation)
    lane = lax.broadcasted_iota(jnp.int32, stats.shape[1:], 1)
    stats[0] = jnp.where(
        lane == 0, count, jnp.where(lane == 1, sum_here, jnp.where(lane == 2, squares, 0.0))
    )

    def st_copy(k):
        peer = lax.rem(me + k, everyone)
        return pltpu.make_async_remote_copy(
            src_ref=stats.at[0], dst_ref=stats.at[k], send_sem=st_send.at[k],
            recv_sem=st_recv.at[k],
            device_id={"tile": peer // orients, "orient": lax.rem(peer, orients)},
            device_id_type=MESH,
        )

    def st_start(k, carry):
        st_copy(k).start()
        return carry

    def st_wait(k, carry):
        st_copy(k).wait()
        return carry

    lax.fori_loop(1, everyone, st_start, 0)
    lax.fori_loop(1, everyone, st_wait, 0)
    table = stats[:, 0, :]
    counts, sums, sqs = table[:, 0:1], table[:, 1:2], table[:, 2:3]
    live = jnp.sum(counts, axis=0, keepdims=True)
    average = jnp.sum(sums, axis=0, keepdims=True) / live
    gap = sums / jnp.maximum(counts, 1.0) - average
    variance = jnp.sum(sqs + counts * gap * gap, axis=0, keepdims=True) / live
    out[...] = unmasked * (lse - average) / jnp.sqrt(variance + 1e-05)


def body(tiles, orients, micrograph, templates, orient_ids, log_weight, ice_mask):
    extent, side = micrograph.shape
    patch = templates.shape[2]
    share = side // orients
    blocks = side // patch
    everyone = tiles * orients
    vmem = pl.BlockSpec(memory_space=pltpu.VMEM)
    smem = pl.BlockSpec(memory_space=pltpu.SMEM)
    dma = pltpu.SemaphoreType.DMA
    consts = [jnp.asarray(table) for table in tables(patch)]
    return pl.pallas_call(
        functools.partial(kernel, tiles, orients, patch // 2),
        out_shape=jax.ShapeDtypeStruct((share, side), F32),
        in_specs=[vmem, vmem, smem, smem, vmem] + [vmem] * len(consts),
        out_specs=vmem,
        scratch_shapes=[
            pltpu.VMEM((extent, patch), F32),
            pltpu.VMEM((extent, patch), F32),
            pltpu.VMEM((tiles, patch, patch), F32),
            pltpu.VMEM((tiles, 8, 128), F32),
            pltpu.VMEM((blocks, 4 * patch, side), F32),
            pltpu.VMEM((8, 128), F32),
            pltpu.VMEM((tiles, side, side), F32),
            pltpu.VMEM((orients, share, side), F32),
            pltpu.VMEM((orients, share, side), F32),
            pltpu.VMEM((everyone, 8, 128), F32),
            dma((2,)), dma((2,)),
            dma((tiles,)), dma((tiles,)), dma((tiles,)), dma((tiles,)),
            dma((orients,)), dma((orients,)),
            dma((everyone,)), dma((everyone,)),
        ],
        compiler_params=pltpu.CompilerParams(
            collective_id=0, has_side_effects=True, vmem_limit_bytes=56 * 1024 * 1024
        ),
    )(micrograph, templates, orient_ids, log_weight, ice_mask, *consts)


def solution(mesh):
    return jax.shard_map(
        functools.partial(body, mesh.shape["tile"], mesh.shape["orient"]),
        mesh=mesh,
        in_specs=(
            P("group", "tile"),
            P("orient", "tile", None, None),
            P("orient", "tile"),
            P(),
            P("group", "tile"),
        ),
        out_specs=P(("group", "orient"), "tile"),
        check_vma=False,
    )
```

profile of v0, /device:TPU:0, one launch (start us, length us, event | category | flops | bytes accessed | tf_op | source)
XLA Modules:
  0.0 37.6 jit_solution(6178090962282156105)
XLA Ops:
  0.7 35.5 %shard_map.100 = f32[64,256]{1,0:T(8,128)} custom-call(f32[384,256]{1,0:T(8,128)} %mic.1, f32[1,1,128,128]{3,2,1,0:T(8,128)} %tpl.1, s32[1,1]{1,0:T(1,128)S(6)} %copy.12.ids, f32[16]{0:T(128)} %logw.1, s32[16,16]{1,0:T(8,128)} %mask.1, bf16[512,256]{1,0:T(8,128)(2,1)} %constant.10.clone.tx, bf16[512,128]{1,0:T(8,128)(2,1)} %constant.11.clone.ix, ...), custom_call_target="tpu_custom_call" | custom-call | tf_op jit(solution)/shard_map/pallas_call | solution.py:317
  36.1 1.5 %copy.13 = f32[64,256]{1,0:T(8,128)} copy(f32[64,256]{1,0:T(8,128)} %shard_map.100) | data formatting | bytes 131072
where the time goes:
time: 37.8 us; the launch traced here: 37.6 us
  Pallas kernels  35.5 us (94%)
  local copies, waits for them, and re-layouts  1.47 us (4%)
  between operations  0.66 us (2%)
    pallas_call x1, Pallas kernels, body(): pl.pallas_call(functools.partial(kernel, tiles, orients, patch // 2), out...  35.5 us
    unnamed x1, local copies, waits for them, and re-layouts  1.47 us

commit v1 on v0

--- a/solution.py
+++ b/solution.py
@@ -67,9 +67,11 @@
 
 def kernel(
     tiles, orients, guard,
-    mic, tpl, ids, logw, mask, tx, ix, ty, tt, iy,
+    mic, tpl, ids, logw, mask, tx_any, ix_any, ty_any, tt_any, iy_any,
     out,
+    tx, ix, ty, tt, iy, pack_l, pack_r,
     halo_l, halo_r, stack, wbuf, img, spec, scores, lse_out, lse_in, stats,
+    table_sem,
     halo_send, halo_recv, tpl_send, tpl_recv, w_send, w_recv,
     lse_send, lse_recv, st_send, st_recv,
 ):
@@ -96,8 +98,33 @@
 
     lax.fori_loop(1, everyone, greet, 0)
 
-    wbuf[0] = jnp.full(wbuf.shape[1:], logw[ids[0, 0]], F32)
+    loads = {}
+    order = (("tx", tx_any, tx), ("tt", tt_any, tt), ("ty", ty_any, ty), ("ix", ix_any, ix), ("iy", iy_any, iy))
+    for index, (name, source, target) in enumerate(order):
+        loads[name] = pltpu.make_async_copy(source, target, table_sem.at[index])
+        loads[name].start()
+
+    known = lax.broadcasted_iota(jnp.int32, (1, logw.shape[1]), 1) == ids[...]
+    weight = jnp.sum(jnp.where(known, logw[...], 0.0), axis=1, keepdims=True)
+    wbuf[0] = jnp.broadcast_to(weight, wbuf.shape[1:])
     stack[0] = tpl[0, 0]
+
+    middle = extent // 2
+    lane_half = lax.broadcasted_iota(jnp.int32, (middle, patch), 1) < guard
+    outer, inner = mic[:, side - patch:], mic[:, :patch]
+    pack_r[...] = jnp.where(lane_half, pltpu.roll(outer[:middle], guard, 1), outer[middle:])
+    pack_l[...] = jnp.where(lane_half, inner[:middle], pltpu.roll(inner[middle:], guard, 1))
+
+    loads["tx"].wait()
+    loads["tt"].wait()
+    tx_head = jnp.concatenate([tx[:patch, :], tx[length:length + patch, :]], axis=0)
+
+    def spectrum(k):
+        half = right_table(stack[k], tx_head)
+        high, low = split(jnp.concatenate([half[:, :patch], half[:, patch:]], axis=0))
+        spec[k] = left_table(tt, high, low)
+
+    spectrum(0)
 
     pl.semaphore_wait(barrier, everyone - 1)
 
@@ -107,8 +134,8 @@
             recv_sem=halo_recv.at[side_index], device_id={"tile": peer}, device_id_type=MESH,
         )
 
-    to_right = halo_copy(mic.at[:, side - patch:], halo_l, 0, lax.rem(t + 1, tiles))
-    to_left = halo_copy(mic.at[:, :patch], halo_r, 1, lax.rem(t + tiles - 1, tiles))
+    to_right = halo_copy(pack_r, halo_l, 0, lax.rem(t + 1, tiles))
+    to_left = halo_copy(pack_l, halo_r, 1, lax.rem(t + tiles - 1, tiles))
 
     @pl.when(t < tiles - 1)
     def _():
@@ -117,23 +144,31 @@
     @pl.when(t > 0)
     def _():
         to_left.start()
+
+    def partner(k):
+        if tiles & (tiles - 1):
+            return lax.rem(t + k, tiles)
+        bit, peer = 1, 0
+        while bit < tiles:
+            peer = peer + lax.rem(t // bit + k // bit, 2) * bit
+            bit *= 2
+        return peer
 
     def tpl_copy(k):
         return pltpu.make_async_remote_copy(
             src_ref=tpl.at[0, 0], dst_ref=stack.at[k], send_sem=tpl_send.at[k],
-            recv_sem=tpl_recv.at[k], device_id={"tile": lax.rem(t + k, tiles)},
+            recv_sem=tpl_recv.at[k], device_id={"tile": partner(k)},
             device_id_type=MESH,
         )
 
     def w_copy(k):
         return pltpu.make_async_remote_copy(
             src_ref=wbuf.at[0], dst_ref=wbuf.at[k], send_sem=w_send.at[k],
-            recv_sem=w_recv.at[k], device_id={"tile": lax.rem(t + k, tiles)},
+            recv_sem=w_recv.at[k], device_id={"tile": partner(k)},
             device_id_type=MESH,
         )
 
-    for k in range(1, tiles):
-        tpl_copy(k).start()
+    tpl_copy(1).start()
     for k in range(1, tiles):
         w_copy(k).start()
 
@@ -147,6 +182,9 @@
     cols_of = jnp.where((col_id >= col_edge) & (col_id < col_edge + MBLK), 1.0, 0.0).astype(F32)
     unmasked = 1.0 - dot(dot(rows_of, mask[...].astype(F32)), cols_of)
 
+    tpl_copy(1).wait()
+    spectrum(1)
+
     @pl.when(t < tiles - 1)
     def _():
         to_right.wait_send()
@@ -165,8 +203,16 @@
     def _():
         halo_l[...] = jnp.zeros(halo_l.shape, F32)
 
-    rolled = [halo_l[...]] + [mic[:, b * patch:(b + 1) * patch] for b in range(blocks)] + [halo_r[...]]
-    rolled = [pltpu.roll(part, guard, 1) for part in rolled]
+    for k in range(2, tiles):
+        tpl_copy(k).start()
+
+    left, right = halo_l[...], halo_r[...]
+    rolled = [pltpu.roll(mic[:, b * patch:(b + 1) * patch], guard, 1) for b in range(blocks)]
+    rolled = (
+        [jnp.concatenate([left, pltpu.roll(left, guard, 1)], axis=0)]
+        + rolled
+        + [jnp.concatenate([pltpu.roll(right, guard, 1), right], axis=0)]
+    )
     lane = lax.broadcasted_iota(jnp.int32, (extent, patch), 1)
     ext = [jnp.where(lane < guard, rolled[b], rolled[b + 1]) for b in range(blocks + 1)]
     real, imag = [], []
@@ -176,6 +222,7 @@
         imag.append(half[:, patch:])
     real_high, real_low = split(jnp.concatenate(real, axis=1))
     imag_high, imag_low = split(jnp.concatenate(imag, axis=1))
+    loads["ty"].wait()
     for a in range(blocks):
         rows = slice(a * patch, a * patch + length)
         img[a] = left_table(
@@ -184,56 +231,34 @@
             jnp.concatenate([real_low[rows], imag_low[rows]], axis=0),
         )
 
-    tx_head = jnp.concatenate([tx[:patch, :], tx[length:length + patch, :]], axis=0)
-
-    def one_template(k):
-        half = right_table(stack[k], tx_head)
-        high, low = split(jnp.concatenate([half[:, :patch], half[:, patch:]], axis=0))
-        sp = left_table(tt, high, low)
-        sr, si = sp[:length], sp[length:]
+    loads["ix"].wait()
+    loads["iy"].wait()
+
+    def correlate(k, a):
+        sr, si = spec[k, :length], spec[k, length:]
         wide_r = jnp.concatenate([sr] * blocks, axis=1)
         wide_i = jnp.concatenate([si] * blocks, axis=1)
         weight = wbuf[k][:1, :1]
-        for a in range(blocks):
-            ir, ii = img[a, :length, :], img[a, length:, :]
-            cross = jnp.concatenate([ir * wide_r + ii * wide_i, ii * wide_r - ir * wide_i], axis=0)
-            high, low = split(cross)
-            mid = left_table(iy, high, low)
-            pieces = jnp.concatenate(
-                [
-                    jnp.concatenate(
-                        [mid[:patch, b * patch:(b + 1) * patch], mid[patch:, b * patch:(b + 1) * patch]],
-                        axis=1,
-                    )
-                    for b in range(blocks)
-                ],
-                axis=0,
-            )
-            final = right_table(pieces, ix) + weight
-            for b in range(blocks):
-                scores[k, a * patch:(a + 1) * patch, b * patch:(b + 1) * patch] = final[
-                    b * patch:(b + 1) * patch
-                ]
-
-    if tiles <= 4:
-        for k in range(tiles):
-            if k:
-                tpl_copy(k).wait()
-                w_copy(k).wait()
-            one_template(k)
-    else:
-        for k in range(1, tiles):
-            tpl_copy(k).wait()
-            w_copy(k).wait()
-
-        def step(k, carry):
-            one_template(k)
-            return carry
-
-        lax.fori_loop(0, tiles, step, 0)
-
-    def own_lse(owner):
-        rows = pl.ds(pl.multiple_of(owner * share, share), share)
+        ir, ii = img[a, :length, :], img[a, length:, :]
+        cross = jnp.concatenate([ir * wide_r + ii * wide_i, ii * wide_r - ir * wide_i], axis=0)
+        high, low = split(cross)
+        mid = left_table(iy, high, low)
+        pieces = jnp.concatenate(
+            [
+                jnp.concatenate(
+                    [mid[:patch, b * patch:(b + 1) * patch], mid[patch:, b * patch:(b + 1) * patch]],
+                    axis=1,
+                )
+                for b in range(blocks)
+            ],
+            axis=0,
+        )
+        final = right_table(pieces, ix) + weight
+        for b in range(blocks):
+            scores[k, :, b * patch:(b + 1) * patch] = final[b * patch:(b + 1) * patch]
+
+    def own_lse(place):
+        rows = pl.ds(pl.multiple_of(place * share, share), share)
         top = scores[0, rows, :]
         for k in range(1, tiles):
             top = jnp.maximum(top, scores[k, rows, :])
@@ -249,10 +274,49 @@
             device_id_type=MESH,
         )
 
-    for k in range(1, orients):
-        lse_out[k] = own_lse(lax.rem(o + k, orients))
-        lse_copy(k).start()
-    mine = own_lse(o)
+    owners = patch // share
+    home, seat = o // owners, lax.rem(o, owners)
+
+    def send_rows(a, place):
+        ahead = lax.rem(a * owners + place - o + orients, orients)
+        lse_out[ahead] = own_lse(place)
+        lse_copy(ahead).start()
+
+    for s in range(blocks):
+        a = lax.rem(home + 1 + s, blocks)
+        if tiles <= 4:
+            for k in range(tiles):
+                if s == 0 and k:
+                    w_copy(k).wait()
+                if s == 0 and k > 1:
+                    tpl_copy(k).wait()
+                    spectrum(k)
+                correlate(k, a)
+        else:
+            if s == 0:
+                w_copy(1).wait()
+                for k in range(2, tiles):
+                    tpl_copy(k).wait()
+                    w_copy(k).wait()
+
+                def later(k, carry):
+                    spectrum(k)
+                    return carry
+
+                lax.fori_loop(2, tiles, later, 0)
+
+            def step(k, carry):
+                correlate(k, a)
+                return carry
+
+            lax.fori_loop(0, tiles, step, 0)
+        if s < blocks - 1:
+            for place in range(owners):
+                send_rows(a, place)
+        else:
+            for gap in range(1, owners):
+                send_rows(a, lax.rem(seat + gap, owners))
+    mine = own_lse(seat)
     for k in range(1, orients):
         lse_copy(k).wait()
     top = mine
@@ -311,25 +375,28 @@
     blocks = side // patch
     everyone = tiles * orients
     vmem = pl.BlockSpec(memory_space=pltpu.VMEM)
-    smem = pl.BlockSpec(memory_space=pltpu.SMEM)
     dma = pltpu.SemaphoreType.DMA
     consts = [jnp.asarray(table) for table in tables(patch)]
     return pl.pallas_call(
         functools.partial(kernel, tiles, orients, patch // 2),
         out_shape=jax.ShapeDtypeStruct((share, side), F32),
-        in_specs=[vmem, vmem, smem, smem, vmem] + [vmem] * len(consts),
+        in_specs=[vmem] * 5 + [pl.BlockSpec(memory_space=pl.ANY)] * len(consts),
         out_specs=vmem,
         scratch_shapes=[
-            pltpu.VMEM((extent, patch), F32),
-            pltpu.VMEM((extent, patch), F32),
+            *[pltpu.VMEM(table.shape, BF16) for table in consts],
+            pltpu.VMEM((extent // 2, patch), F32),
+            pltpu.VMEM((extent // 2, patch), F32),
+            pltpu.VMEM((extent // 2, patch), F32),
+            pltpu.VMEM((extent // 2, patch), F32),
             pltpu.VMEM((tiles, patch, patch), F32),
             pltpu.VMEM((tiles, 8, 128), F32),
             pltpu.VMEM((blocks, 4 * patch, side), F32),
-            pltpu.VMEM((8, 128), F32),
-            pltpu.VMEM((tiles, side, side), F32),
+            pltpu.VMEM((tiles, 4 * patch, patch), F32),
+            pltpu.VMEM((tiles, patch, side), F32),
             pltpu.VMEM((orients, share, side), F32),
             pltpu.VMEM((orients, share, side), F32),
             pltpu.VMEM((everyone, 8, 128), F32),
+            dma((len(consts),)),
             dma((2,)), dma((2,)),
             dma((tiles,)), dma((tiles,)), dma((tiles,)), dma((tiles,)),
             dma((orients,)), dma((orients,)),
@@ -338,7 +405,7 @@
         compiler_params=pltpu.CompilerParams(
             collective_id=0, has_side_effects=True, vmem_limit_bytes=56 * 1024 * 1024
         ),
-    )(micrograph, templates, orient_ids, log_weight, ice_mask, *consts)
+    )(micrograph, templates, orient_ids, log_weight.reshape(1, -1), ice_mask, *consts)
 
 
 def solution(mesh):

time: 37.8 us -> 32.3 us (0.85)
  Pallas kernels: 35.5 us -> 30 us
    pallas_call x1, Pallas kernels: 35.5 us -> 30 us  [body(): pl.pallas_call(functools.partial(kernel, tiles, orients, patch // 2), out...]
where the time goes in v1:
time: 32.3 us; the launch traced here: 32.1 us
  Pallas kernels  30 us (93%)
  local copies, waits for them, and re-layouts  1.47 us (5%)
  between operations  0.66 us (2%)
    pallas_call x1, Pallas kernels, body(): pl.pallas_call(functools.partial(kernel, tiles, orients, patch // 2), out...  30 us
    unnamed x1, local copies, waits for them, and re-layouts  1.47 us

profile of v1, /device:TPU:0, one launch (start us, length us, event | category | flops | bytes accessed | tf_op | source)
XLA Modules:
  0.0 32.1 jit_solution(1886019724474874889)
XLA Ops:
  0.7 30.0 %shard_map.100 = f32[64,256]{1,0:T(8,128)} custom-call(f32[384,256]{1,0:T(8,128)} %mic.1, f32[1,1,128,128]{3,2,1,0:T(8,128)} %tpl.1, s32[1,1]{1,0:T(1,128)S(6)} %copy.12.ids, f32[1,16]{1,0:T(1,128)} %bitcast.1, s32[16,16]{1,0:T(8,128)} %mask.1, bf16[512,256]{1,0:T(8,128)(2,1)} %constant.10.clone.tx_any, bf16[512,128]{1,0:T(8,128)(2,1)} %constant.11.clone.ix_any, ...), custom_call_target="tpu_custom_call" | custom-call | tf_op jit(solution)/shard_map/pallas_call | solution.py:380
  30.7 1.5 %copy.13 = f32[64,256]{1,0:T(8,128)} copy(f32[64,256]{1,0:T(8,128)} %shard_map.100) | data formatting | bytes 131072

commit v2 on v1

--- a/solution.py
+++ b/solution.py
@@ -395,7 +395,7 @@
             pltpu.VMEM((tiles, patch, side), F32),
             pltpu.VMEM((orients, share, side), F32),
             pltpu.VMEM((orients, share, side), F32),
-            pltpu.VMEM((everyone, 8, 128), F32),
+            pltpu.VMEM((everyone, 1, 128), F32),
             dma((len(consts),)),
             dma((2,)), dma((2,)),
             dma((tiles,)), dma((tiles,)), dma((tiles,)), dma((tiles,)),

time: 32.3 us -> 32.1 us (level)
  no operation moved by 1% of the time
where the time goes in v2:
time: 32.1 us; the launch traced here: 31.9 us
  Pallas kernels  29.8 us (93%)
  local copies, waits for them, and re-layouts  1.47 us (5%)
  between operations  0.66 us (2%)
    pallas_call x1, Pallas kernels, body(): pl.pallas_call(functools.partial(kernel, tiles, orients, patch // 2), out...  29.8 us
    unnamed x1, local copies, waits for them, and re-layouts  1.47 us

profile of v2, /device:TPU:0, one launch (start us, length us, event | category | flops | bytes accessed | tf_op | source)
XLA Modules:
  0.0 31.9 jit_solution(2039172069824239547)
XLA Ops:
  0.7 29.8 %shard_map.100 = f32[64,256]{1,0:T(8,128)} custom-call(f32[384,256]{1,0:T(8,128)} %mic.1, f32[1,1,128,128]{3,2,1,0:T(8,128)} %tpl.1, s32[1,1]{1,0:T(1,128)S(6)} %copy.12.ids, f32[1,16]{1,0:T(1,128)} %bitcast.1, s32[16,16]{1,0:T(8,128)} %mask.1, bf16[512,256]{1,0:T(8,128)(2,1)} %constant.10.clone.tx_any, bf16[512,128]{1,0:T(8,128)(2,1)} %constant.11.clone.ix_any, ...), custom_call_target="tpu_custom_call" | custom-call | tf_op jit(solution)/shard_map/pallas_call | solution.py:380
  30.4 1.5 %copy.13 = f32[64,256]{1,0:T(8,128)} copy(f32[64,256]{1,0:T(8,128)} %shard_map.100) | data formatting | bytes 131072
